TPU v7x, 32 devices: a whole 2x2x4 slice. The times are simulated.
32 devices in a mesh: query: 4 (over y, x), cand: 2 (over core), tensor: 4 (over z).
Axes of the slice: x: 2, y: 2, z: 4, core: 2. Of those that a mesh axis runs over, the one named last changes fastest.
Arguments:
- cand_states: bfloat16 [8192, 2048], P(('query', 'cand'), 'tensor'), parts along dimension 0, may hold values from -6 to 6
- prefix_states: bfloat16 [256, 2048], P(('query', 'cand'), 'tensor'), parts along dimension 0, may hold values from -6 to 6
- norm_gain: float32 [2048], replicated, may hold values from 0.5 to 1.5
- w_query: bfloat16 [2048, 1024], P(None, 'tensor'), may hold values from -1 to 1
- w_key: bfloat16 [2048, 256], P(None, 'tensor'), may hold values from -1 to 1
- w_value: bfloat16 [2048, 256], P(None, 'tensor'), may hold values from -0.125 to 0.125
- w_out: bfloat16 [1024, 2048], P('tensor'), may hold values from -1.5 to 1.5
- cand_lengths: int32 [64], P(('query', 'cand')), parts along dimension 0, may hold values from 32 to 128, as said below
Outputs:
- attn_out: bfloat16 [8192, 2048], P(('query', 'cand', 'tensor')), parts along dimension 0
There are 4 independent parts, one for each index of `query`. A program takes and returns all parts, laid end to end along the dimension named above; an argument that names none is the same for every part. Nothing has to cross between parts.
Inputs may be any that keep to these rules, and one draw needn't show every extreme that they name: `cand_lengths`: some candidate has all 128 slots live.
All inputs are finite; a program needn't handle non-finite values.
Results may differ from a plain program's by a relative error of at most 0.013.
Values may be sent and summed in bfloat16 or wider, within the bound.
No kernel may reach another device: no remote copies, remote signals or barrier semaphores. Data moves between devices by JAX's collectives and lax.ppermute only.
A program may use at most 64 MiB of HBM per device.

v0:
```python
import jax
import jax.numpy as jnp
from jax import lax
from jax.sharding import PartitionSpec as P

epsilon = 1e-06
theta_base = 10000.0


def rotate(values, positions):
    half_size = values.shape[-1] // 2
    frequency = theta_base ** (-jnp.arange(half_size, dtype=jnp.float32) * 2.0 / values.shape[-1])
    angles = positions.astype(jnp.float32)[:, None] * frequency[None, :]
    cosine = jnp.cos(angles)
    sine_part = jnp.sin(angles)
    lower_half = values[:, :half_size]
    upper_half = values[:, half_size:]
    return jnp.concatenate(
        [
            lower_half * cosine - upper_half * sine_part,
            upper_half * cosine + lower_half * sine_part,
        ],
        axis=-1,
    )


def normalize(states, norm_gain):
    values = states.astype(jnp.float32)
    square = jnp.mean(values * values, axis=-1, keepdims=True)
    return (values * lax.rsqrt(square + epsilon) * norm_gain[None, :]).astype(jnp.bfloat16)


def self_scores_of(queries, cand_keys):
    scores = jnp.einsum("cqd,ckd->cqk", queries, cand_keys, preferred_element_type=jnp.float32)
    slots = jnp.arange(scores.shape[1], dtype=jnp.int32)
    causal = slots[:, None] >= slots[None, :]
    return jnp.where(causal[None], scores, -jnp.inf)


def body(cand_states, prefix_states, norm_gain, w_query, w_key, w_value, w_out, cand_lengths):
    cand_full, prefix_full = (
        lax.all_gather(cand_states, "tensor", axis=1, tiled=True),
        lax.all_gather(prefix_states, "tensor", axis=1, tiled=True),
    )
    normed_cand = normalize(cand_full, norm_gain)
    normed_prefix = normalize(prefix_full, norm_gain)
    cand_count = cand_lengths.shape[0]
    cand_len = cand_full.shape[0] // cand_count
    prefix_rows = prefix_full.shape[0]
    cand_groups = lax.axis_size("cand")
    tensor_size = lax.axis_size("tensor")
    prefix_len = prefix_rows * cand_groups
    head_size = w_query.shape[1]
    cand_pos = prefix_len + jnp.tile(jnp.arange(cand_len, dtype=jnp.int32), cand_count)
    cand_key = jnp.dot(normed_cand, w_key, preferred_element_type=jnp.float32).astype(jnp.bfloat16)
    cand_value = jnp.dot(normed_cand, w_value, preferred_element_type=jnp.float32).astype(
        jnp.bfloat16
    )
    prefix_key = jnp.dot(normed_prefix, w_key, preferred_element_type=jnp.float32).astype(
        jnp.bfloat16
    )
    prefix_value = jnp.dot(normed_prefix, w_value, preferred_element_type=jnp.float32).astype(
        jnp.bfloat16
    )
    query_rows = rotate(
        jnp.dot(normed_cand, w_query, preferred_element_type=jnp.float32), cand_pos
    ) * head_size ** (-0.5)
    queries = query_rows.astype(jnp.bfloat16).reshape(cand_count, cand_len, head_size)
    cand_key, cand_value = (
        lax.all_gather(cand_key, "tensor", axis=1, tiled=True),
        lax.all_gather(cand_value, "tensor", axis=1, tiled=True),
    )
    key_pieces, value_pieces = (
        lax.all_gather(prefix_key, ("cand", "tensor"), axis=0, tiled=True),
        lax.all_gather(prefix_value, ("cand", "tensor"), axis=0, tiled=True),
    )

    def arrange(pieces):
        blocks = pieces.reshape(cand_groups, tensor_size, prefix_rows, pieces.shape[1])
        return blocks.transpose(0, 2, 1, 3).reshape(prefix_len, pieces.shape[1] * tensor_size)

    prefix_pos = jnp.arange(prefix_len, dtype=jnp.int32)
    prefix_keys = rotate(arrange(key_pieces).astype(jnp.float32), prefix_pos).astype(jnp.bfloat16)
    prefix_values = arrange(value_pieces)
    cand_keys = (
        rotate(cand_key.astype(jnp.float32), cand_pos)
        .astype(jnp.bfloat16)
        .reshape(cand_count, cand_len, head_size)
    )
    cand_values = cand_value.reshape(cand_count, cand_len, head_size)
    self_scores = self_scores_of(queries, cand_keys)
    prefix_scores = jnp.einsum(
        "cqd,kd->cqk", queries, prefix_keys, preferred_element_type=jnp.float32
    )
    highest = jnp.maximum(self_scores.max(-1), prefix_scores.max(-1))
    self_weights = jnp.exp(self_scores - highest[..., None])
    prefix_weights = jnp.exp(prefix_scores - highest[..., None])
    divisor = self_weights.sum(-1) + prefix_weights.sum(-1)
    summed = jnp.einsum(
        "cqk,ckd->cqd",
        self_weights.astype(jnp.bfloat16),
        cand_values,
        preferred_element_type=jnp.float32,
    )
    summed = summed + jnp.einsum(
        "cqk,kd->cqd",
        prefix_weights.astype(jnp.bfloat16),
        prefix_values,
        preferred_element_type=jnp.float32,
    )
    slots = jnp.arange(cand_len, dtype=jnp.int32)
    live_rows = slots[None, :] < cand_lengths[:, None]
    head_rows = jnp.where(live_rows[..., None], summed / divisor[..., None], 0.0)
    head_rows = head_rows.reshape(cand_count * cand_len, head_size).astype(jnp.bfloat16)
    row_count = head_rows.shape[0] // tensor_size
    all_heads = lax.all_to_all(head_rows, "tensor", split_axis=0, concat_axis=1, tiled=True)
    full_out = lax.all_gather(w_out, "tensor", axis=0, tiled=True)
    summed_out = jnp.zeros((row_count, full_out.shape[1]), jnp.float32)
    for head_index in range(tensor_size):
        head_term = jnp.dot(
            all_heads[:, head_index * head_size : (head_index + 1) * head_size],
            full_out[head_index * head_size : (head_index + 1) * head_size],
            preferred_element_type=jnp.float32,
        )
        summed_out = summed_out + lax.optimization_barrier(head_term.astype(jnp.bfloat16)).astype(
            jnp.float32
        )
    return summed_out.astype(jnp.bfloat16)


def solution(mesh):
    in_specs = (
        P(("query", "cand"), "tensor"),
        P(("query", "cand"), "tensor"),
        P(),
        P(None, "tensor"),
        P(None, "tensor"),
        P(None, "tensor"),
        P("tensor", None),
        P(("query", "cand")),
    )
    out_specs = P(("query", "cand", "tensor"), None)
    return jax.shard_map(body, mesh=mesh, in_specs=in_specs, out_specs=out_specs, check_vma=False)
```

profile of v0, /device:TPU:0, one launch (start us, length us, event | category | flops | bytes accessed | tf_op | source)
XLA Modules:
  0.0 214.7 jit_solution(11699257511544938787)
XLA Ops:
  6.5 0.0 copy-start
  6.5 0.0 all-gather.3.cloned.1.call-start
  6.5 0.7 all-gather.3.cloned.1.call-update
  7.3 0.0 all-gather.5.cloned.1.call-start
  7.3 0.7 all-gather.5.cloned.1.call-update
  8.0 15.3 %all_gather.23 = bf16[32,2048]{1,0:T(8,128)(2,1)S(1)} all-gather(bf16[32,512]{1,0:T(8,128)(2,1)} %param.9), channel_id=1, replica_groups=mesh['query'=4,'cand'=2,'tensor'=4] {'tensor'}, dimensions={1}, use_global_device_ids=true | all-gather | bytes 163840 | tf_op jit(solution)/shard_map/all_gather | solution.py:43
  23.3 0.1 fusion.30
  23.5 1.2 convolution_convert_fusion.7
  24.7 26.7 %all_gather.24 = bf16[256,64]{1,0:T(8,128)(2,1)S(1)} all-gather(bf16[32,64]{1,0:T(8,128)(2,1)S(1)} %convolution_convert_fusion.7), channel_id=1, replica_groups=mesh['query'=4,'cand'=2,'tensor'=4] {'cand','tensor'}, dimensions={0}, use_global_device_ids=true | all-gather | bytes 36864 | tf_op jit(solution)/shard_map/all_gather | solution.py:74
  51.4 0.1 copy.21
  51.5 0.1 reshape.111
  51.6 1.2 convolution_convert_fusion.6
  52.8 27.9 %all_gather.26 = bf16[256,64]{1,0:T(8,128)(2,1)S(1)} all-gather(bf16[32,64]{1,0:T(8,128)(2,1)S(1)} %convolution_convert_fusion.6), channel_id=1, replica_groups=mesh['query'=4,'cand'=2,'tensor'=4] {'cand','tensor'}, dimensions={0}, use_global_device_ids=true | all-gather | bytes 36864 | tf_op jit(solution)/shard_map/all_gather | solution.py:75
  80.8 0.1 reshape.114
  81.0 0.0 copy-done.7
  81.0 0.1 iota_compare_fusion.1
  81.1 0.2 fusion.51
  81.3 13.3 %all-gather.3.cloned.1.call-done = bf16[1024,2048]{1,0:T(8,128)(2,1)} async-done(((bf16[1024,512]{1,0:T(8,128)(2,1)}), bf16[1024,2048]{1,0:T(8,128)(2,1)}) %all-gather.3.cloned.1.call-update) | async-done | bytes 4194320 | tf_op jit(solution)/shard_map/all_gather | solution.py:42
  94.6 3.2 %fusion = f32[1024]{0:T(1024)S(1)} fusion(bf16[1024,2048]{1,0:T(8,128)(2,1)} %all-gather.3.cloned.1.call-done), kind=kLoop, calls=%fused_computation.2 | loop fusion | flops 6290432 | bytes 4198400 | tf_op jit(solution)/shard_map/reduce_sum | solution.py:29
  97.8 0.0 copy-done.6
  97.8 0.2 copy-done.2
  98.0 1.0 fusion.2
  99.0 0.0 copy-start.1
  99.1 2.0 copy-done.1
  101.0 1.4 convolution_convert_fusion.5
  102.4 21.4 %all_gather.22 = bf16[1024,256]{0,1:T(8,128)(2,1)S(1)} all-gather(bf16[1024,64]{0,1:T(8,128)(2,1)S(1)} %convolution_convert_fusion.5), channel_id=1, replica_groups=mesh['query'=4,'cand'=2,'tensor'=4] {'tensor'}, dimensions={1}, use_global_device_ids=true | all-gather | bytes 655360 | tf_op jit(solution)/shard_map/all_gather | solution.py:70
  123.8 0.2 copy.20
  124.0 0.1 convert_element_type.144
  124.1 3.6 %convolution_convert_fusion.4 = bf16[1024,64]{0,1:T(8,128)(2,1)S(1)} fusion(bf16[1024,2048]{1,0:T(8,128)(2,1)} %copy-done.1, bf16[2048,64]{0,1:T(8,128)(2,1)S(1)} %copy-done.5), kind=kOutput, calls=%fused_computation.15 | convolution fusion | flops 268500992 | bytes 4587520 | tf_op jit(solution)/shard_map/dot_general | solution.py:56
  127.7 21.3 %all_gather.25 = bf16[1024,256]{0,1:T(8,128)(2,1)S(1)} all-gather(bf16[1024,64]{0,1:T(8,128)(2,1)S(1)} %convolution_convert_fusion.4), channel_id=1, replica_groups=mesh['query'=4,'cand'=2,'tensor'=4] {'tensor'}, dimensions={1}, use_global_device_ids=true | all-gather | bytes 655360 | tf_op jit(solution)/shard_map/all_gather | solution.py:71
  149.0 0.2 copy.27
  149.2 3.5 %fusion.67 = f32[1024,256]{1,0:T(8,128)S(1)} fusion(bf16[1024,2048]{1,0:T(8,128)(2,1)} %copy-done.1, bf16[2048,256]{1,0:T(8,128)(2,1)S(1)} %copy-done), kind=kOutput, calls=%fused_computation.92 | convolution fusion | flops 1073741824 | bytes 6291456 | tf_op jit(solution)/shard_map/dot_general | solution.py:66
  152.7 2.5 %fusion.19 = (f32[1024,128]{1,0:T(8,128)S(1)}, f32[1024,128]{1,0:T(8,128)S(1)}, bf16[1024,128]{1,0:T(8,128)(2,1)S(1)}, bf16[1024,128]{1,0:T(8,128)(2,1)S(1)}) fusion(f32[1024,256]{1,0:T(8,128)S(1)} %fusion.67, f32[128]{0:T(128)S(1)} %multiply_power_fusion, f32[1024]{0:T(1024)S(1)} %convert_bitcast_fusion.1, f32[1024,256]{1,0:T(8,128)S(1)} %convert_element_type.144), kind=kLoop, calls=%fused_computation.35 | loop fusion | flops 1966080 | bytes 3674624 | tf_op jit(solution)/shard_map/sub | solution.py:20
  155.2 0.3 fusion.66
  155.5 0.3 fusion.65
  155.8 0.1 fusion.36
  155.9 0.1 fusion.28
  156.0 0.3 fusion.33
  156.3 0.4 fusion.5
  156.8 1.0 copy.25
  157.8 5.3 %all-to-all-start = ((bf16[4,256,256]{1,2,0:T(8,128)(2,1)}), bf16[4,256,256]{1,2,0:T(8,128)(2,1)S(1)}, u32[]{:S(2)}, u32[]{:S(2)}) async-start(bf16[4,256,256]{1,2,0:T(8,128)(2,1)} %copy.25), calls=%async_computation | async-start | bytes 1048576 | tf_op jit(solution)/shard_map/all_to_all | solution.py:116
  163.1 38.6 %all-gather.5.cloned.1.call-done = bf16[1024,2048]{1,0:T(8,128)(2,1)} async-done(((bf16[256,2048]{1,0:T(8,128)(2,1)}), bf16[1024,2048]{1,0:T(8,128)(2,1)}) %all-gather.5.cloned.1.call-update) | async-done | bytes 4194320 | tf_op jit(solution)/shard_map/all_gather | solution.py:117
  201.7 0.0 all-to-all-done
  201.7 1.8 convolution_convert_fusion.3
  203.6 1.7 convolution_convert_fusion.2
  205.3 0.5 convolution_convert_fusion.1
  205.7 0.5 convolution_convert_fusion
  206.2 1.7 add_convert_fusion
  (20 shorter events, 0.1 us)
Async XLA Ops:
  6.5 142.7 %copy-start = (bf16[2048,256]{1,0:T(8,128)(2,1)S(1)}, bf16[2048,256]{1,0:T(8,128)(2,1)}, u32[]{:S(2)}) copy-start(bf16[2048,256]{1,0:T(8,128)(2,1)} %param.11) | copy-start | bytes 3145732
  6.5 91.3 %copy-start.6 = (f32[2048]{0:T(1024)S(1)}, f32[2048]{0:T(1024)}, u32[]{:S(2)}) copy-start(f32[2048]{0:T(1024)} %param.10) | copy-start | bytes 24580
  6.5 74.5 %copy-start.7 = (s32[8]{0:T(128)S(1)}, s32[8]{0:T(128)}, u32[]{:S(2)}) copy-start(s32[8]{0:T(128)} %param.15) | copy-start | bytes 100
  6.5 88.0 %all-gather.3.cloned.1.call-start = ((), (), s32[]{:S(2)}) async-start(), calls=%async_computation.1 | async-start | bytes 5242880 | tf_op jit(solution)/shard_map/all_gather | solution.py:42
  7.3 194.5 %all-gather.5.cloned.1.call-start = ((), (), s32[]{:S(2)}) async-start(), calls=%async_computation.2 | async-start | bytes 5242880 | tf_op jit(solution)/shard_map/all_gather | solution.py:117
  94.6 3.4 %copy-start.2 = (bf16[1024,2048]{1,0:T(8,128)(2,1)S(1)}, bf16[1024,2048]{1,0:T(8,128)(2,1)}, u32[]{:S(2)}) copy-start(bf16[1024,2048]{1,0:T(8,128)(2,1)} %all-gather.3.cloned.1.call-done) | copy-start | bytes 12582916
  98.0 3.0 %copy-start.4 = (bf16[2048,64]{0,1:T(8,128)(2,1)S(1)}, bf16[2048,64]{0,1:T(8,128)(2,1)}, u32[]{:S(2)}) copy-start(bf16[2048,64]{0,1:T(8,128)(2,1)} %param.12) | copy-start | bytes 786436
  99.0 2.0 copy-start.1
  101.0 23.0 %copy-start.5 = (bf16[2048,64]{0,1:T(8,128)(2,1)S(1)}, bf16[2048,64]{0,1:T(8,128)(2,1)}, u32[]{:S(2)}) copy-start(bf16[2048,64]{0,1:T(8,128)(2,1)} %param.13) | copy-start | bytes 786436
  157.8 44.0 %all-to-all-start = ((bf16[4,256,256]{1,2,0:T(8,128)(2,1)}), bf16[4,256,256]{1,2,0:T(8,128)(2,1)S(1)}, u32[]{:S(2)}, u32[]{:S(2)}) async-start(bf16[4,256,256]{1,2,0:T(8,128)(2,1)} %copy.25), calls=%async_computation | async-start | bytes 1048576 | tf_op jit(solution)/shard_map/all_to_all | solution.py:116
  201.7 3.5 %copy-start.3 = (bf16[1024,2048]{1,0:T(8,128)(2,1)S(1)}, bf16[1024,2048]{1,0:T(8,128)(2,1)}, u32[]{:S(2)}) copy-start(bf16[1024,2048]{1,0:T(8,128)(2,1)} %all-gather.5.cloned.1.call-done) | copy-start | bytes 12582916
Sparse Core Ops, SparseCore 0:
  8.9 85.6 all-gather.2
  96.1 105.5 all-gather.4
where the time goes:
time: 215 us
  blocking collectives  113 us (53%)
  waiting for transfers between devices  53.3 us (25%)
  matrix products  16.8 us (8%)
  between operations  13.6 us (6%)
  other arithmetic  9.09 us (4%)
  starting transfers between devices  5.36 us (2%)
  local copies, waits for them, and re-layouts  3.97 us (2%)
    all_gather x1, waiting for transfers between devices, body(): full_out = lax.all_gather(w_out, 'tensor', axis=0, tiled=True)  38.6 us
    all_gather x1, blocking collectives, body(): lax.all_gather(prefix_value, ('cand', 'tensor'), axis=0, tiled=True)  27.9 us
    all_gather x1, blocking collectives, body(): lax.all_gather(prefix_key, ('cand', 'tensor'), axis=0, tiled=True)  26.7 us
    all_gather x1, blocking collectives, body(): lax.all_gather(cand_key, 'tensor', axis=1, tiled=True)  21.4 us
    all_gather x1, blocking collectives, body(): lax.all_gather(cand_value, 'tensor', axis=1, tiled=True)  21.3 us
    all_gather x1, blocking collectives, body(): lax.all_gather(prefix_states, 'tensor', axis=1, tiled=True)  15.3 us
    all_gather x1, waiting for transfers between devices, body(): lax.all_gather(cand_states, 'tensor', axis=1, tiled=True)  13.3 us
    all_to_all x1, starting transfers between devices, body(): lax.all_to_all(head_rows, 'tensor', split_axis=0, concat_axis=1, tiled=True)  5.32 us
  transfers between devices with their start and end apart: 3, of which 2 were waited for; matrix products, arithmetic and copies ran while one was open for 10% of the time, Pallas kernels for 0%

commit v1 on v0

v1 whole, which is shorter than its diff:
```python
import functools

import jax
import jax.numpy as jnp
from jax import lax
from jax.experimental import pallas as pl
from jax.experimental.pallas import tpu as pltpu
from jax.sharding import PartitionSpec as P


epsilon = 1e-06
theta_base = 10000.0
PLANE = ("query", "cand")


def shift(k):
    n = lax.axis_size("tensor")
    return lambda v: lax.ppermute(v, "tensor", [(i, (i + k) % n) for i in range(n)])


def other_core(v):
    n = lax.axis_size("cand")
    return lax.ppermute(v, "cand", [(i, i ^ 1) for i in range(n)])


def plane_xor(masks):
    nq, nc = lax.axis_size("query"), lax.axis_size("cand")
    pairs = [(q * nc + c, (q ^ masks[c % 2]) * nc + c) for q in range(nq) for c in range(nc)]
    return lambda v: lax.ppermute(v, PLANE, pairs)


def spread(piece):
    bits = lax.axis_size("query").bit_length() - 1
    held = [(piece, (0, 0))]
    for step in range(bits):
        flip = (1 << step, 1 << ((step + 1) % bits))
        held = held + [
            (
                plane_xor(flip)(v),
                (masks[0] ^ flip[0], masks[1] ^ flip[1]),
            )
            for v, masks in held
        ]
    crossed = [(other_core(v), (masks[1], masks[0]), 1) for v, masks in held]
    return [(v, masks, 0) for v, masks in held] + crossed


def rotary_tables(count, half, head_size):
    frequency = theta_base ** (-jnp.arange(half, dtype=jnp.float32) * 2.0 / head_size)
    angles = jnp.arange(count, dtype=jnp.float32)[:, None] * frequency[None, :]
    return jnp.cos(angles), jnp.sin(angles)


def kernel(dims, plan, *refs):
    n, rows, cand_len, prefix_len, depth, head, out_cols = dims
    n_in = 9 + (n - 1) + sum(len(p) for p in plan)
    cand_ref, prefix_ref, gain_ref, cos_ref, sin_ref, len_ref = refs[:6]
    own_q, own_kv, own_out = refs[6:9]
    x_refs = refs[9 : 9 + n - 1]
    piece_refs = refs[9 + n - 1 : n_in]
    o_ref = refs[n_in]
    x_raw, normed, w_in, w_fin, q_scr, kv_scr, heads, sems = refs[n_in + 1 :]
    me = lax.axis_index("tensor")
    q_at = lax.axis_index("query")
    parity = lax.rem(lax.axis_index("cand"), 2)
    width = depth // n
    kv_cols = own_kv.shape[1]
    in_cols = head + kv_cols
    half = head // 2
    share = kv_cols // 2

    count = 0

    def copy(src, dst):
        nonlocal count
        c = pltpu.make_async_copy(src, dst, sems.at[count])
        count += 1
        c.start()
        return c

    def source(k):
        return lax.rem(me - k + n, n)

    x_copies = []
    for k in range(n):
        lanes = pl.ds(pl.multiple_of(source(k) * width, width), width)
        src = cand_ref.at[pl.ds(pl.multiple_of(me * rows, rows), rows), :] if k == 0 else x_refs[k - 1]
        x_copies.append(copy(src, x_raw.at[pl.ds(0, rows), lanes]))
        x_copies.append(copy(prefix_ref.at[k], x_raw.at[pl.ds(rows, prefix_len), lanes]))
    in_copies = [[copy(own_q, w_in.at[0, :, pl.ds(0, head)]), copy(own_kv, w_in.at[0, :, pl.ds(head, kv_cols)])]]
    fin_copies = [[copy(own_out, w_fin.at[0])]]
    at = 0
    where = []
    for k in range(1, n):
        here, later = [], []
        for masks, crossed in plan[k - 1]:
            mask = jnp.where(parity == 0, masks[0], masks[1])
            part = lax.bitwise_xor(q_at, mask) * 2 + (parity if not crossed else 1 - parity)
            ref = piece_refs[at]
            at += 1
            size = ref.shape[0]
            start = pl.multiple_of(part * size, size)
            here.append(copy(ref.at[:, pl.ds(0, in_cols)], w_in.at[k, pl.ds(start, size), :]))
            later.append((ref, start, size))
        in_copies.append(here)
        where.append(later)
    for k in range(1, n):
        fin_copies.append(
            [
                copy(ref.at[:, pl.ds(in_cols, size)], w_fin.at[k, :, pl.ds(start, size)])
                for ref, start, size in where[k - 1]
            ]
        )

    for c in x_copies:
        c.wait()
    block = 32
    gain = gain_ref[...]

    @pl.loop(0, (rows + prefix_len) // block)
    def _(i):
        at_rows = pl.ds(pl.multiple_of(i * block, block), block)
        values = x_raw[at_rows, :].astype(jnp.float32)
        square = jnp.mean(values * values, axis=-1, keepdims=True)
        normed[at_rows, :] = (values * lax.rsqrt(square + epsilon) * gain).astype(jnp.bfloat16)

    cos, sin = cos_ref[...], sin_ref[...]
    cand_cos = jnp.concatenate([cos[prefix_len:]] * (rows // cand_len), axis=0)
    cand_sin = jnp.concatenate([sin[prefix_len:]] * (rows // cand_len), axis=0)

    for k in range(n):
        for c in in_copies[k]:
            c.wait()
        made = jnp.dot(normed[...], w_in[k], preferred_element_type=jnp.float32)
        lower, upper = made[:rows, :half], made[:rows, half:head]
        scale = head ** (-0.5)
        q_scr[k, :, :half] = ((lower * cand_cos - upper * cand_sin) * scale).astype(jnp.bfloat16)
        q_scr[k, :, half:] = ((upper * cand_cos + lower * cand_sin) * scale).astype(jnp.bfloat16)
        kv_scr[source(k)] = made[:, head:].astype(jnp.bfloat16)

    pieces = [kv_scr[s] for s in range(n)]
    low = jnp.concatenate([p[:, :share] for p in pieces[: n // 2]], axis=1).astype(jnp.float32)
    up = jnp.concatenate([p[:, :share] for p in pieces[n // 2 :]], axis=1).astype(jnp.float32)
    all_cos = jnp.concatenate([cand_cos, cos[:prefix_len]], axis=0)
    all_sin = jnp.concatenate([cand_sin, sin[:prefix_len]], axis=0)
    keys = jnp.concatenate(
        [low * all_cos - up * all_sin, up * all_cos + low * all_sin], axis=1
    ).astype(jnp.bfloat16)
    values = jnp.concatenate([p[:, share:] for p in pieces], axis=1)
    prefix_keys, prefix_values = keys[rows:], values[rows:]

    rows_at = lax.broadcasted_iota(jnp.int32, (cand_len, cand_len), 0)
    cols_at = lax.broadcasted_iota(jnp.int32, (cand_len, cand_len), 1)
    causal = rows_at >= cols_at
    slot = lax.broadcasted_iota(jnp.int32, (cand_len, 1), 0)
    trans = (((1,), (1,)), ((), ()))
    for j in range(rows // cand_len):
        own = slice(j * cand_len, (j + 1) * cand_len)
        live = slot < len_ref[me * (rows // cand_len) + j]
        keys_j, values_j = keys[own], values[own]
        for k in range(n):
            queries = q_scr[k, own, :]
            self_s = lax.dot_general(queries, keys_j, trans, preferred_element_type=jnp.float32)
            self_s = jnp.where(causal, self_s, -jnp.inf)
            pre_s = lax.dot_general(queries, prefix_keys, trans, preferred_element_type=jnp.float32)
            top = jnp.maximum(self_s.max(-1, keepdims=True), pre_s.max(-1, keepdims=True))
            self_w = jnp.exp(self_s - top)
            pre_w = jnp.exp(pre_s - top)
            divisor = self_w.sum(-1, keepdims=True) + pre_w.sum(-1, keepdims=True)
            mix = jnp.dot(self_w.astype(jnp.bfloat16), values_j, preferred_element_type=jnp.float32)
            mix = mix + jnp.dot(
                pre_w.astype(jnp.bfloat16), prefix_values, preferred_element_type=jnp.float32
            )
            heads[k, own, :] = jnp.where(live, mix / divisor, 0.0).astype(jnp.bfloat16)

    for group in fin_copies:
        for c in group:
            c.wait()
    tile = min(512, out_cols)
    for col in range(0, out_cols, tile):
        total = None
        for k in range(n):
            term = jnp.dot(
                heads[k], w_fin[k, :, col : col + tile], preferred_element_type=jnp.float32
            )
            term = term.astype(jnp.bfloat16).astype(jnp.float32)
            total = term if total is None else total + term
        o_ref[:, col : col + tile] = total.astype(jnp.bfloat16)


def body(cand_states, prefix_states, norm_gain, w_query, w_key, w_value, w_out, cand_lengths):
    n = lax.axis_size("tensor")
    nq, nc = lax.axis_size("query"), lax.axis_size("cand")
    me = lax.axis_index("tensor")
    part = lax.axis_index("query") * 2 + lax.axis_index("cand") % 2
    depth, head = w_query.shape
    out_cols = w_out.shape[1]
    size = depth // (2 * nq)
    cand_len = cand_states.shape[0] // cand_lengths.shape[0]
    rows = cand_states.shape[0] // n
    prefix_len = prefix_states.shape[0] * nc
    half = head // 2

    def take(v, at, size, axis):
        return lax.dynamic_slice_in_dim(v, at * size, size, axis)

    own_kv = jnp.concatenate([w_key, w_value], axis=1)
    piece = jnp.concatenate(
        [
            take(w_query, part, size, 0),
            take(w_key, part, size, 0),
            take(w_value, part, size, 0),
            take(w_out, part, size, 1),
        ],
        axis=1,
    )
    moved = {1: shift(1)(piece)}
    if n > 2:
        moved[n - 1] = shift(n - 1)(piece)
    for k in range(2, n - 1):
        moved[k] = shift(1)(moved[k - 1])
    pre = [prefix_states] + [shift(k)(prefix_states) for k in range(1, n)]
    xs = [shift(k)(take(cand_states, (me + k) % n, rows, 0)) for k in range(1, n)]
    pre = jnp.stack(pre)
    if nc == 2:
        far = other_core(pre)
        even = lax.axis_index("cand") == 0
        pre = jnp.where(
            even, jnp.concatenate([pre, far], axis=1), jnp.concatenate([far, pre], axis=1)
        )
    else:
        pre = lax.all_gather(pre, "cand", axis=1, tiled=True)
    spreads = [spread(moved[k]) for k in range(1, n)]
    plan = tuple(tuple((masks, crossed) for _, masks, crossed in s) for s in spreads)
    pieces = [v for s in spreads for v, _, _ in s]
    cos, sin = rotary_tables(prefix_len + cand_len, half, head)

    dims = (n, rows, cand_len, prefix_len, depth, head, out_cols)
    any_spec = pl.BlockSpec(memory_space=pl.ANY)
    vmem = pl.BlockSpec(memory_space=pltpu.VMEM)
    smem = pl.BlockSpec(memory_space=pltpu.SMEM)
    kv_cols = own_kv.shape[1]
    return pl.pallas_call(
        functools.partial(kernel, dims, plan),
        name="main",
        out_shape=jax.ShapeDtypeStruct((rows, out_cols), jnp.bfloat16),
        in_specs=[any_spec, any_spec, vmem, vmem, vmem, smem]
        + [any_spec] * (3 + len(xs) + len(pieces)),
        out_specs=vmem,
        scratch_shapes=[
            pltpu.VMEM((rows + prefix_len, depth), jnp.bfloat16),
            pltpu.VMEM((rows + prefix_len, depth), jnp.bfloat16),
            pltpu.VMEM((n, depth, head + kv_cols), jnp.bfloat16),
            pltpu.VMEM((n, head, out_cols), jnp.bfloat16),
            pltpu.VMEM((n, rows, head), jnp.bfloat16),
            pltpu.VMEM((n, rows + prefix_len, kv_cols), jnp.bfloat16),
            pltpu.VMEM((n, rows, head), jnp.bfloat16),
            pltpu.SemaphoreType.DMA((2 * n + 3 + 2 * len(pieces),)),
        ],
        compiler_params=pltpu.CompilerParams(vmem_limit_bytes=40 * 2**20),
    )(
        cand_states, pre, norm_gain.reshape(1, depth), cos, sin, cand_lengths,
        w_query, own_kv, w_out, *xs, *pieces,
    )


def solution(mesh):
    in_specs = (
        P(("query", "cand"), "tensor"),
        P(("query", "cand"), "tensor"),
        P(),
        P(None, "tensor"),
        P(None, "tensor"),
        P(None, "tensor"),
        P("tensor", None),
        P(("query", "cand")),
    )
    out_specs = P(("query", "cand", "tensor"), None)

    return jax.shard_map(body, mesh=mesh, in_specs=in_specs, out_specs=out_specs, check_vma=False)
```

time: 215 us -> 100 us (0.47)
  blocking collectives: 113 us -> 0 us
  starting transfers between devices: 5.36 us -> 25.5 us
  matrix products: 16.8 us -> 0 us
  between operations: 13.6 us -> 0.3 us
  Pallas kernels: 0 us -> 10.3 us
  local copies, waits for them, and re-layouts: 3.97 us -> 10.6 us
  waiting for transfers between devices: 53.3 us -> 48.6 us
  other arithmetic: 9.09 us -> 4.58 us
    all_gather x5 -> x0, blocking collectives: 113 us -> none  [the longest x1 27.9 us: body(): lax.all_gather(prefix_value, ('cand', 'tensor'), axis=0, tiled=True)]
    all_gather x2 -> x0, waiting for transfers between devices: 51.9 us -> none  [the longest x1 38.6 us: body(): full_out = lax.all_gather(w_out, 'tensor', axis=0, tiled=True)]
    ppermute x0 -> x31, waiting for transfers between devices: none -> 48.6 us  [the longest x9 31.3 us: shift(): lax.ppermute(v, 'tensor', [(i, (i + k) % n) for i in range(n)])]
    ppermute x0 -> x31, starting transfers between devices: none -> 25.5 us  [the longest x9 13.9 us: shift(): lax.ppermute(v, 'tensor', [(i, (i + k) % n) for i in range(n)])]
    dot_general x13 -> x0, matrix products: 16.8 us -> none  [the longest x4 4.42 us: body(): jnp.dot(all_heads[:, head_index * head_size:(head_index + 1) * head_size]...]
    pallas_call x0 -> x1, Pallas kernels: none -> 10.3 us  [body(): pl.pallas_call(functools.partial(kernel, dims, plan), name='main', out_sh...]
    unnamed x16 -> x46, local copies, waits for them, and re-layouts: 2.19 us -> 9.47 us
    all_to_all x1 -> x0, starting transfers between devices: 5.32 us -> none  [body(): lax.all_to_all(head_rows, 'tensor', split_axis=0, concat_axis=1, tiled=True)]
  transfers between devices with their start and end apart: 3 -> 31, of which waited for: 2 -> 10; matrix products, arithmetic and copies ran while one was open for 10% -> 8% of each run, Pallas kernels for 0% -> 0%
where the time goes in v1:
time: 100 us; the launch traced here: 99.9 us
  waiting for transfers between devices  48.6 us (49%)
  starting transfers between devices  25.5 us (26%)
  local copies, waits for them, and re-layouts  10.6 us (11%)
  Pallas kernels  10.3 us (10%)
  other arithmetic  4.58 us (5%)
    ppermute x9, waiting for transfers between devices, shift(): lax.ppermute(v, 'tensor', [(i, (i + k) % n) for i in range(n)])  31.3 us
    ppermute x9, waiting for transfers between devices, plane_xor(): return lambda v: lax.ppermute(v, PLANE, pairs)  17 us
    ppermute x9, starting transfers between devices, shift(): lax.ppermute(v, 'tensor', [(i, (i + k) % n) for i in range(n)])  13.9 us
    pallas_call x1, Pallas kernels, body(): pl.pallas_call(functools.partial(kernel, dims, plan), name='main', out_sh...  10.3 us
    ppermute x9, starting transfers between devices, plane_xor(): return lambda v: lax.ppermute(v, PLANE, pairs)  10.2 us
    unnamed x46, local copies, waits for them, and re-layouts  9.47 us
  transfers between devices with their start and end apart: 31, of which 10 were waited for; matrix products, arithmetic and copies ran while one was open for 8% of the time, Pallas kernels for 0%

profile of v1, /device:TPU:0, one launch (start us, length us, event | category | flops | bytes accessed | tf_op | source)
XLA Modules:
  0.0 99.9 jit_solution(9351026822052574344)
XLA Ops:
  0.0 3.1 %collective-permute-start = (bf16[32,512]{1,0:T(8,128)(2,1)}, bf16[32,512]{1,0:T(8,128)(2,1)S(1)}, u32[]{:S(2)}, u32[]{:S(2)}) collective-permute-start(bf16[32,512]{1,0:T(8,128)(2,1)} %param.9), channel_id=1, source_target_pairs={{0,1},{1,2},{2,3},{3,0},{4,5},{5,6},{6,7},{7,4},{8,9},{9,10},{10,1... | collective-permute-start | bytes 98312 | tf_op jit(solution)/shard_map/ppermute | solution.py:18
  3.1 2.1 %collective-permute-start.2 = (bf16[32,512]{1,0:T(8,128)(2,1)}, bf16[32,512]{1,0:T(8,128)(2,1)S(1)}, u32[]{:S(2)}, u32[]{:S(2)}) collective-permute-start(bf16[32,512]{1,0:T(8,128)(2,1)} %param.9), channel_id=1, source_target_pairs={{0,3},{1,0},{2,1},{3,2},{4,7},{5,4},{6,5},{7,6},{8,11},{9,8},{10,9... | collective-permute-start | bytes 98312 | tf_op jit(solution)/shard_map/ppermute | solution.py:18
  5.1 1.0 collective-permute-start.1
  6.1 1.2 %copy.9 = bf16[2048,64]{1,0:T(8,128)(2,1)S(1)} copy(bf16[2048,64]{0,1:T(8,128)(2,1)} %param.12) | data formatting | bytes 524288 | tf_op args[4]
  7.3 1.4 %copy.10 = bf16[2048,64]{1,0:T(8,128)(2,1)S(1)} copy(bf16[2048,64]{0,1:T(8,128)(2,1)} %param.13) | data formatting | bytes 524288 | tf_op args[5]
  8.8 1.1 %constant_dynamic-slice_fusion = (bf16[256,256]{1,0:T(8,128)(2,1)S(1)}, bf16[256,256]{1,0:T(8,128)(2,1)S(1)}) fusion(bf16[256,2048]{1,0:T(8,128)(2,1)} %refs_8_.1, s32[]{:T(128)S(6)} %select_n.51, bf16[2048,256]{1,0:T(8,128)(2,1)S(1)} %copy-done.1), kind=kLoop, calls=%fused_computation.7 | loop fusion | bytes 524292 | tf_op jit(solution)/shard_map/dynamic_slice | solution.py:205
  9.9 0.8 pad_maximum_fusion.1
  10.8 1.3 %collective-permute-start.23 = (bf16[256,640]{1,0:T(8,128)(2,1)}, bf16[256,640]{1,0:T(8,128)(2,1)S(1)}, u32[]{:S(2)}, u32[]{:S(2)}) collective-permute-start(bf16[256,640]{1,0:T(8,128)(2,1)} %pad_maximum_fusion.1), channel_id=1, source_target_pairs={{0,3},{1,0},{2,1},{3,2},{4,7},{5,4},{6,5},{7,6},{8,11},{9,8},{10,9... | collective-permute-start | bytes 983048 | tf_op jit(solution)/shard_map/ppermute | solution.py:18
  12.2 2.1 %collective-permute-start.6 = (bf16[256,512]{1,0:T(8,128)(2,1)S(1)}, bf16[256,512]{1,0:T(8,128)(2,1)S(1)}, u32[]{:S(2)}, u32[]{:S(2)}) collective-permute-start(bf16[256,512]{1,0:T(8,128)(2,1)S(1)} %get-tuple-element.5), channel_id=1, source_target_pairs={{0,3},{1,0},{2,1},{3,2},{4,7},{5,4},{6,5},{7,6},{8,11},{9,8},{10,9... | collective-permute-start | bytes 786440 | tf_op jit(solution)/shard_map/ppermute | solution.py:18
  14.4 0.6 copy-done.20
  15.0 0.8 pad_maximum_fusion.2
  15.8 0.1 collective-permute-start.3
  15.9 5.6 %collective-permute-done.23.refs_28_ = bf16[256,640]{1,0:T(8,128)(2,1)S(1)} collective-permute-done((bf16[256,640]{1,0:T(8,128)(2,1)}, bf16[256,640]{1,0:T(8,128)(2,1)S(1)}, u32[]{:S(2)}, u32[]{:S(2)}) %collective-permute-start.23) | collective-permute-done | bytes 327712 | tf_op jit(solution)/shard_map/ppermute | solution.py:18
  21.6 1.5 %collective-permute-start.25 = (bf16[256,640]{1,0:T(8,128)(2,1)S(1)}, bf16[256,640]{1,0:T(8,128)(2,1)S(1)}, u32[]{:S(2)}, u32[]{:S(2)}) collective-permute-start(bf16[256,640]{1,0:T(8,128)(2,1)S(1)} %collective-permute-done.23.refs_28_), channel_id=1, source_target_pairs={{0,16},{4,12},{8,24},{12,4},{16,0},{20,28},{24,8},{28,20},{1,17},{... | collective-permute-start | bytes 983048 | tf_op jit(solution)/shard_map/ppermute | solution.py:29
  23.1 2.1 %collective-permute-start.5 = (bf16[256,512]{1,0:T(8,128)(2,1)S(1)}, bf16[256,512]{1,0:T(8,128)(2,1)S(1)}, u32[]{:S(2)}, u32[]{:S(2)}) collective-permute-start(bf16[256,512]{1,0:T(8,128)(2,1)S(1)} %get-tuple-element.6), channel_id=1, source_target_pairs={{0,2},{1,3},{2,0},{3,1},{4,6},{5,7},{6,4},{7,5},{8,10},{9,11},{10,... | collective-permute-start | bytes 786440 | tf_op jit(solution)/shard_map/ppermute | solution.py:18
  25.2 0.9 collective-permute-done.6.refs_11_
  26.1 0.7 copy-done.9
  26.8 2.2 %collective-permute-start.4 = (bf16[256,512]{1,0:T(8,128)(2,1)S(1)}, bf16[256,512]{1,0:T(8,128)(2,1)S(1)}, u32[]{:S(2)}, u32[]{:S(2)}) collective-permute-start(bf16[256,512]{1,0:T(8,128)(2,1)S(1)} %get-tuple-element.7), channel_id=1, source_target_pairs={{0,1},{1,2},{2,3},{3,0},{4,5},{5,6},{6,7},{7,4},{8,9},{9,10},{10,1... | collective-permute-start | bytes 786440 | tf_op jit(solution)/shard_map/ppermute | solution.py:18
  29.0 21.1 %collective-permute-done.5.refs_10_ = bf16[256,512]{1,0:T(8,128)(2,1)S(1)} collective-permute-done((bf16[256,512]{1,0:T(8,128)(2,1)S(1)}, bf16[256,512]{1,0:T(8,128)(2,1)S(1)}, u32[]{:S(2)}, u32[]{:S(2)}) %collective-permute-start.5) | collective-permute-done | bytes 262176 | tf_op jit(solution)/shard_map/ppermute | solution.py:18
  50.1 0.7 copy-done.11
  50.8 1.5 %collective-permute-start.24 = (bf16[256,640]{1,0:T(8,128)(2,1)S(1)}, bf16[256,640]{1,0:T(8,128)(2,1)}, u32[]{:S(2)}, u32[]{:S(2)}) collective-permute-start(bf16[256,640]{1,0:T(8,128)(2,1)S(1)} %collective-permute-done.23.refs_28_), channel_id=1, source_target_pairs={{0,8},{4,20},{8,0},{12,28},{16,24},{20,4},{24,16},{28,12},{1,9},{5... | collective-permute-start | bytes 983048 | tf_op jit(solution)/shard_map/ppermute | solution.py:29
  52.3 0.7 copy-done.13
  53.1 1.5 %collective-permute-start.9 = (bf16[256,640]{1,0:T(8,128)(2,1)S(1)}, bf16[256,640]{1,0:T(8,128)(2,1)S(1)}, u32[]{:S(2)}, u32[]{:S(2)}) collective-permute-start(bf16[256,640]{1,0:T(8,128)(2,1)S(1)} %collective-permute-done.7.refs_12_), channel_id=1, source_target_pairs={{0,16},{4,12},{8,24},{12,4},{16,0},{20,28},{24,8},{28,20},{1,17},{... | collective-permute-start | bytes 983048 | tf_op jit(solution)/shard_map/ppermute | solution.py:29
  54.6 0.5 collective-permute-start.8
  55.1 4.6 %collective-permute-done.24.refs_29_ = bf16[256,640]{1,0:T(8,128)(2,1)} collective-permute-done((bf16[256,640]{1,0:T(8,128)(2,1)S(1)}, bf16[256,640]{1,0:T(8,128)(2,1)}, u32[]{:S(2)}, u32[]{:S(2)}) %collective-permute-start.24) | collective-permute-done | bytes 327712 | tf_op jit(solution)/shard_map/ppermute | solution.py:29
  59.7 3.6 %collective-permute-done.15.refs_20_ = bf16[256,640]{1,0:T(8,128)(2,1)} collective-permute-done((bf16[256,640]{1,0:T(8,128)(2,1)S(1)}, bf16[256,640]{1,0:T(8,128)(2,1)}, u32[]{:S(2)}, u32[]{:S(2)}) %collective-permute-start.15) | collective-permute-done | bytes 327712 | tf_op jit(solution)/shard_map/ppermute | solution.py:18
  63.4 0.7 copy-done.3
  64.1 0.6 collective-permute-start.26
  64.7 0.6 collective-permute-start.19
  65.4 0.7 copy-done.7
  66.1 1.0 %collective-permute-start.16 = (bf16[256,640]{1,0:T(8,128)(2,1)}, bf16[256,640]{1,0:T(8,128)(2,1)}, u32[]{:S(2)}, u32[]{:S(2)}) collective-permute-start(bf16[256,640]{1,0:T(8,128)(2,1)} %collective-permute-done.15.refs_20_), channel_id=1, source_target_pairs={{0,8},{4,20},{8,0},{12,28},{16,24},{20,4},{24,16},{28,12},{1,9},{5... | collective-permute-start | bytes 983048 | tf_op jit(solution)/shard_map/ppermute | solution.py:29
  67.1 1.5 %collective-permute-start.17 = (bf16[256,640]{1,0:T(8,128)(2,1)}, bf16[256,640]{1,0:T(8,128)(2,1)S(1)}, u32[]{:S(2)}, u32[]{:S(2)}) collective-permute-start(bf16[256,640]{1,0:T(8,128)(2,1)} %collective-permute-done.15.refs_20_), channel_id=1, source_target_pairs={{0,16},{4,12},{8,24},{12,4},{16,0},{20,28},{24,8},{28,20},{1,17},{... | collective-permute-start | bytes 983048 | tf_op jit(solution)/shard_map/ppermute | solution.py:29
  68.7 4.6 %collective-permute-done.26.refs_31_ = bf16[256,640]{1,0:T(8,128)(2,1)} collective-permute-done((bf16[256,640]{1,0:T(8,128)(2,1)}, bf16[256,640]{1,0:T(8,128)(2,1)}, u32[]{:S(2)}, u32[]{:S(2)}) %collective-permute-start.26) | collective-permute-done | bytes 327712 | tf_op jit(solution)/shard_map/ppermute | solution.py:29
  73.3 0.6 collective-permute-start.10
  73.9 3.1 %collective-permute-done.16.refs_21_ = bf16[256,640]{1,0:T(8,128)(2,1)} collective-permute-done((bf16[256,640]{1,0:T(8,128)(2,1)}, bf16[256,640]{1,0:T(8,128)(2,1)}, u32[]{:S(2)}, u32[]{:S(2)}) %collective-permute-start.16) | collective-permute-done | bytes 327712 | tf_op jit(solution)/shard_map/ppermute | solution.py:29
  77.0 1.4 %collective-permute-start.18 = (bf16[256,640]{1,0:T(8,128)(2,1)}, bf16[256,640]{1,0:T(8,128)(2,1)S(1)}, u32[]{:S(2)}, u32[]{:S(2)}) collective-permute-start(bf16[256,640]{1,0:T(8,128)(2,1)} %collective-permute-done.16.refs_21_), channel_id=1, source_target_pairs={{0,16},{4,12},{8,24},{12,4},{16,0},{20,28},{24,8},{28,20},{1,17},{... | collective-permute-start | bytes 983048 | tf_op jit(solution)/shard_map/ppermute | solution.py:29
  78.5 1.6 %pad_maximum_fusion.refs_7_ = bf16[2048,128]{1,0:T(8,128)(2,1)S(1)} fusion(bf16[2048,64]{1,0:T(8,128)(2,1)} %copy-done.18, bf16[2048,64]{1,0:T(8,128)(2,1)} %copy-done.17), kind=kLoop, calls=%fused_computation | loop fusion | flops 1048576 | bytes 1048576 | tf_op jit(solution)/shard_map/concatenate | solution.py:207
  80.2 0.5 collective-permute-start.30
  80.7 0.1 collective-permute-start.21
  80.8 1.1 %collective-permute-done.10.refs_15_ = bf16[256,640]{1,0:T(8,128)(2,1)S(1)} collective-permute-done((bf16[256,640]{1,0:T(8,128)(2,1)}, bf16[256,640]{1,0:T(8,128)(2,1)S(1)}, u32[]{:S(2)}, u32[]{:S(2)}) %collective-permute-start.10) | collective-permute-done | bytes 327712 | tf_op jit(solution)/shard_map/ppermute | solution.py:29
  81.9 3.5 %collective-permute-done.18.refs_23_ = bf16[256,640]{1,0:T(8,128)(2,1)S(1)} collective-permute-done((bf16[256,640]{1,0:T(8,128)(2,1)}, bf16[256,640]{1,0:T(8,128)(2,1)S(1)}, u32[]{:S(2)}, u32[]{:S(2)}) %collective-permute-start.18) | collective-permute-done | bytes 327712 | tf_op jit(solution)/shard_map/ppermute | solution.py:29
  85.4 0.4 fusion
  85.8 0.9 maximum_select_fusion.refs_1_
  86.8 0.3 collective-permute-done.22.refs_27_
  87.1 0.6 copy-done.16
  87.7 0.9 copy-done.12
  88.7 0.9 copy-done.14
  89.6 10.3 %main.1 = bf16[256,2048]{1,0:T(8,128)(2,1)} custom-call(bf16[1024,512]{1,0:T(8,128)(2,1)S(1)} %copy-done, bf16[4,64,512]{2,1,0:T(8,128)(2,1)S(1)} %maximum_select_fusion.refs_1_, f32[1,2048]{1,0:T(1,128)S(1)} %bitcast.5, f32[192,128]{1,0:T(8,128)S(1)} %get-tuple-element.9.refs_3_, f32[192,128]{1,0:T(8,128)S(1)} %get-tuple-element.8.refs_4_, ...), custom_call_target="tpu_custom_call" | custom-call | tf_op jit(solution)/shard_map/main/pallas_call | solution.py:243
  (70 shorter events, 0.5 us)
Async XLA Ops:
  0.0 8.8 %copy-start.1 = (bf16[2048,256]{1,0:T(8,128)(2,1)S(1)}, bf16[2048,256]{1,0:T(8,128)(2,1)}, u32[]{:S(2)}) copy-start(bf16[2048,256]{1,0:T(8,128)(2,1)} %refs_6_.1) | copy-start | bytes 3145732
  0.0 14.3 %collective-permute-start = (bf16[32,512]{1,0:T(8,128)(2,1)}, bf16[32,512]{1,0:T(8,128)(2,1)S(1)}, u32[]{:S(2)}, u32[]{:S(2)}) collective-permute-start(bf16[32,512]{1,0:T(8,128)(2,1)} %param.9), channel_id=1, source_target_pairs={{0,1},{1,2},{2,3},{3,0},{4,5},{5,6},{6,7},{7,4},{8,9},{9,10},{10,1... | collective-permute-start | bytes 98312 | tf_op jit(solution)/shard_map/ppermute | solution.py:18
  3.1 11.3 %collective-permute-start.2 = (bf16[32,512]{1,0:T(8,128)(2,1)}, bf16[32,512]{1,0:T(8,128)(2,1)S(1)}, u32[]{:S(2)}, u32[]{:S(2)}) collective-permute-start(bf16[32,512]{1,0:T(8,128)(2,1)} %param.9), channel_id=1, source_target_pairs={{0,3},{1,0},{2,1},{3,2},{4,7},{5,4},{6,5},{7,6},{8,11},{9,8},{10,9... | collective-permute-start | bytes 98312 | tf_op jit(solution)/shard_map/ppermute | solution.py:18
  5.1 9.2 %collective-permute-start.1 = (bf16[32,512]{1,0:T(8,128)(2,1)}, bf16[32,512]{1,0:T(8,128)(2,1)}, u32[]{:S(2)}, u32[]{:S(2)}) collective-permute-start(bf16[32,512]{1,0:T(8,128)(2,1)} %param.9), channel_id=1, source_target_pairs={{0,2},{1,3},{2,0},{3,1},{4,6},{5,7},{6,4},{7,5},{8,10},{9,11},{10,... | collective-permute-start | bytes 98312 | tf_op jit(solution)/shard_map/ppermute | solution.py:18
  7.3 2.6 %copy-start.17 = (bf16[2048,64]{1,0:T(8,128)(2,1)}, bf16[2048,64]{1,0:T(8,128)(2,1)S(1)}, u32[]{:S(2)}) copy-start(bf16[2048,64]{1,0:T(8,128)(2,1)S(1)} %copy.9) | copy-start | bytes 786436
  7.3 4.8 %copy-start = (bf16[1024,512]{1,0:T(8,128)(2,1)S(1)}, bf16[1024,512]{1,0:T(8,128)(2,1)}, u32[]{:S(2)}) copy-start(bf16[1024,512]{1,0:T(8,128)(2,1)} %refs_0_.1) | copy-start | bytes 3145732
  8.8 2.0 %copy-start.18 = (bf16[2048,64]{1,0:T(8,128)(2,1)}, bf16[2048,64]{1,0:T(8,128)(2,1)S(1)}, u32[]{:S(2)}) copy-start(bf16[2048,64]{1,0:T(8,128)(2,1)S(1)} %copy.10) | copy-start | bytes 786436
  10.8 10.8 %collective-permute-start.23 = (bf16[256,640]{1,0:T(8,128)(2,1)}, bf16[256,640]{1,0:T(8,128)(2,1)S(1)}, u32[]{:S(2)}, u32[]{:S(2)}) collective-permute-start(bf16[256,640]{1,0:T(8,128)(2,1)} %pad_maximum_fusion.1), channel_id=1, source_target_pairs={{0,3},{1,0},{2,1},{3,2},{4,7},{5,4},{6,5},{7,6},{8,11},{9,8},{10,9... | collective-permute-start | bytes 983048 | tf_op jit(solution)/shard_map/ppermute | solution.py:18
  12.1 2.9 %copy-start.19 = (bf16[32,512]{1,0:T(8,128)(2,1)S(1)}, bf16[32,512]{1,0:T(8,128)(2,1)}, u32[]{:S(2)}) copy-start(bf16[32,512]{1,0:T(8,128)(2,1)} %param.9) | copy-start | bytes 98308
  12.2 13.9 %collective-permute-start.6 = (bf16[256,512]{1,0:T(8,128)(2,1)S(1)}, bf16[256,512]{1,0:T(8,128)(2,1)S(1)}, u32[]{:S(2)}, u32[]{:S(2)}) collective-permute-start(bf16[256,512]{1,0:T(8,128)(2,1)S(1)} %get-tuple-element.5), channel_id=1, source_target_pairs={{0,3},{1,0},{2,1},{3,2},{4,7},{5,4},{6,5},{7,6},{8,11},{9,8},{10,9... | collective-permute-start | bytes 786440 | tf_op jit(solution)/shard_map/ppermute | solution.py:18
  15.0 72.1 %copy-start.15 = (f32[2048]{0:T(1024)S(1)}, f32[2048]{0:T(1024)}, u32[]{:S(2)}) copy-start(f32[2048]{0:T(1024)} %param.10) | copy-start | bytes 24580
  15.8 7.3 %collective-permute-start.3 = (bf16[4,32,512]{2,1,0:T(8,128)(2,1)S(1)}, bf16[4,32,512]{2,1,0:T(8,128)(2,1)S(1)}, u32[]{:S(2)}, u32[]{:S(2)}) collective-permute-start(bf16[4,32,512]{2,1,0:T(8,128)(2,1)S(1)} %pad_maximum_fusion.2), channel_id=1, source_target_pairs={{0,4},{4,0},{1,5},{5,1},{2,6},{6,2},{3,7},{7,3},{8,12},{12,8},{9,1... | collective-permute-start | bytes 393224 | tf_op jit(solution)/shard_map/ppermute | solution.py:23
  15.9 36.4 %collective-permute-start.7 = (bf16[256,640]{1,0:T(8,128)(2,1)}, bf16[256,640]{1,0:T(8,128)(2,1)S(1)}, u32[]{:S(2)}, u32[]{:S(2)}) collective-permute-start(bf16[256,640]{1,0:T(8,128)(2,1)} %pad_maximum_fusion.1), channel_id=1, source_target_pairs={{0,1},{1,2},{2,3},{3,0},{4,5},{5,6},{6,7},{7,4},{8,9},{9,10},{10,1... | collective-permute-start | bytes 983048 | tf_op jit(solution)/shard_map/ppermute | solution.py:18
  21.6 31.5 %collective-permute-start.27 = (bf16[256,640]{1,0:T(8,128)(2,1)S(1)}, bf16[256,640]{1,0:T(8,128)(2,1)S(1)}, u32[]{:S(2)}, u32[]{:S(2)}) collective-permute-start(bf16[256,640]{1,0:T(8,128)(2,1)S(1)} %collective-permute-done.23.refs_28_), channel_id=1, source_target_pairs={{0,4},{4,0},{1,5},{5,1},{2,6},{6,2},{3,7},{7,3},{8,12},{12,8},{9,1... | collective-permute-start | bytes 983048 | tf_op jit(solution)/shard_map/ppermute | solution.py:23
  21.6 33.0 %collective-permute-start.25 = (bf16[256,640]{1,0:T(8,128)(2,1)S(1)}, bf16[256,640]{1,0:T(8,128)(2,1)S(1)}, u32[]{:S(2)}, u32[]{:S(2)}) collective-permute-start(bf16[256,640]{1,0:T(8,128)(2,1)S(1)} %collective-permute-done.23.refs_28_), channel_id=1, source_target_pairs={{0,16},{4,12},{8,24},{12,4},{16,0},{20,28},{24,8},{28,20},{1,17},{... | collective-permute-start | bytes 983048 | tf_op jit(solution)/shard_map/ppermute | solution.py:29
  23.1 27.0 %collective-permute-start.5 = (bf16[256,512]{1,0:T(8,128)(2,1)S(1)}, bf16[256,512]{1,0:T(8,128)(2,1)S(1)}, u32[]{:S(2)}, u32[]{:S(2)}) collective-permute-start(bf16[256,512]{1,0:T(8,128)(2,1)S(1)} %get-tuple-element.6), channel_id=1, source_target_pairs={{0,2},{1,3},{2,0},{3,1},{4,6},{5,7},{6,4},{7,5},{8,10},{9,11},{10,... | collective-permute-start | bytes 786440 | tf_op jit(solution)/shard_map/ppermute | solution.py:18
  26.1 0.7 copy-start.9
  26.8 25.5 %collective-permute-start.4 = (bf16[256,512]{1,0:T(8,128)(2,1)S(1)}, bf16[256,512]{1,0:T(8,128)(2,1)S(1)}, u32[]{:S(2)}, u32[]{:S(2)}) collective-permute-start(bf16[256,512]{1,0:T(8,128)(2,1)S(1)} %get-tuple-element.7), channel_id=1, source_target_pairs={{0,1},{1,2},{2,3},{3,0},{4,5},{5,6},{6,7},{7,4},{8,9},{9,10},{10,1... | collective-permute-start | bytes 786440 | tf_op jit(solution)/shard_map/ppermute | solution.py:18
  50.8 8.9 %collective-permute-start.24 = (bf16[256,640]{1,0:T(8,128)(2,1)S(1)}, bf16[256,640]{1,0:T(8,128)(2,1)}, u32[]{:S(2)}, u32[]{:S(2)}) collective-permute-start(bf16[256,640]{1,0:T(8,128)(2,1)S(1)} %collective-permute-done.23.refs_28_), channel_id=1, source_target_pairs={{0,8},{4,20},{8,0},{12,28},{16,24},{20,4},{24,16},{28,12},{1,9},{5... | collective-permute-start | bytes 983048 | tf_op jit(solution)/shard_map/ppermute | solution.py:29
  52.3 11.1 %collective-permute-start.15 = (bf16[256,640]{1,0:T(8,128)(2,1)S(1)}, bf16[256,640]{1,0:T(8,128)(2,1)}, u32[]{:S(2)}, u32[]{:S(2)}) collective-permute-start(bf16[256,640]{1,0:T(8,128)(2,1)S(1)} %collective-permute-done.7.refs_12_), channel_id=1, source_target_pairs={{0,1},{1,2},{2,3},{3,0},{4,5},{5,6},{6,7},{7,4},{8,9},{9,10},{10,1... | collective-permute-start | bytes 983048 | tf_op jit(solution)/shard_map/ppermute | solution.py:18
  52.3 0.7 copy-start.13
  53.0 10.3 %collective-permute-start.11 = (bf16[256,640]{1,0:T(8,128)(2,1)S(1)}, bf16[256,640]{1,0:T(8,128)(2,1)S(1)}, u32[]{:S(2)}, u32[]{:S(2)}) collective-permute-start(bf16[256,640]{1,0:T(8,128)(2,1)S(1)} %collective-permute-done.7.refs_12_), channel_id=1, source_target_pairs={{0,4},{4,0},{1,5},{5,1},{2,6},{6,2},{3,7},{7,3},{8,12},{12,8},{9,1... | collective-permute-start | bytes 983048 | tf_op jit(solution)/shard_map/ppermute | solution.py:23
  53.1 11.6 %collective-permute-start.9 = (bf16[256,640]{1,0:T(8,128)(2,1)S(1)}, bf16[256,640]{1,0:T(8,128)(2,1)S(1)}, u32[]{:S(2)}, u32[]{:S(2)}) collective-permute-start(bf16[256,640]{1,0:T(8,128)(2,1)S(1)} %collective-permute-done.7.refs_12_), channel_id=1, source_target_pairs={{0,16},{4,12},{8,24},{12,4},{16,0},{20,28},{24,8},{28,20},{1,17},{... | collective-permute-start | bytes 983048 | tf_op jit(solution)/shard_map/ppermute | solution.py:29
  54.6 10.8 %collective-permute-start.8 = (bf16[256,640]{1,0:T(8,128)(2,1)S(1)}, bf16[256,640]{1,0:T(8,128)(2,1)S(1)}, u32[]{:S(2)}, u32[]{:S(2)}) collective-permute-start(bf16[256,640]{1,0:T(8,128)(2,1)S(1)} %collective-permute-done.7.refs_12_), channel_id=1, source_target_pairs={{0,8},{4,20},{8,0},{12,28},{16,24},{20,4},{24,16},{28,12},{1,9},{5... | collective-permute-start | bytes 983048 | tf_op jit(solution)/shard_map/ppermute | solution.py:29
  59.7 7.4 %collective-permute-start.29 = (bf16[256,640]{1,0:T(8,128)(2,1)S(1)}, bf16[256,640]{1,0:T(8,128)(2,1)}, u32[]{:S(2)}, u32[]{:S(2)}) collective-permute-start(bf16[256,640]{1,0:T(8,128)(2,1)S(1)} %collective-permute-done.25.refs_30_), channel_id=1, source_target_pairs={{0,4},{4,0},{1,5},{5,1},{2,6},{6,2},{3,7},{7,3},{8,12},{12,8},{9,1... | collective-permute-start | bytes 983048 | tf_op jit(solution)/shard_map/ppermute | solution.py:23
  63.4 5.3 %collective-permute-start.28 = (bf16[256,640]{1,0:T(8,128)(2,1)}, bf16[256,640]{1,0:T(8,128)(2,1)}, u32[]{:S(2)}, u32[]{:S(2)}) collective-permute-start(bf16[256,640]{1,0:T(8,128)(2,1)} %collective-permute-done.24.refs_29_), channel_id=1, source_target_pairs={{0,4},{4,0},{1,5},{5,1},{2,6},{6,2},{3,7},{7,3},{8,12},{12,8},{9,1... | collective-permute-start | bytes 983048 | tf_op jit(solution)/shard_map/ppermute | solution.py:23
  63.4 0.7 copy-start.3
  64.1 9.2 %collective-permute-start.26 = (bf16[256,640]{1,0:T(8,128)(2,1)}, bf16[256,640]{1,0:T(8,128)(2,1)}, u32[]{:S(2)}, u32[]{:S(2)}) collective-permute-start(bf16[256,640]{1,0:T(8,128)(2,1)} %collective-permute-done.24.refs_29_), channel_id=1, source_target_pairs={{0,16},{4,12},{8,24},{12,4},{16,0},{20,28},{24,8},{28,20},{1,17},{... | collective-permute-start | bytes 983048 | tf_op jit(solution)/shard_map/ppermute | solution.py:29
  64.7 9.2 %collective-permute-start.19 = (bf16[256,640]{1,0:T(8,128)(2,1)}, bf16[256,640]{1,0:T(8,128)(2,1)}, u32[]{:S(2)}, u32[]{:S(2)}) collective-permute-start(bf16[256,640]{1,0:T(8,128)(2,1)} %collective-permute-done.15.refs_20_), channel_id=1, source_target_pairs={{0,4},{4,0},{1,5},{5,1},{2,6},{6,2},{3,7},{7,3},{8,12},{12,8},{9,1... | collective-permute-start | bytes 983048 | tf_op jit(solution)/shard_map/ppermute | solution.py:23
  65.4 0.7 copy-start.7
  66.1 10.9 %collective-permute-start.16 = (bf16[256,640]{1,0:T(8,128)(2,1)}, bf16[256,640]{1,0:T(8,128)(2,1)}, u32[]{:S(2)}, u32[]{:S(2)}) collective-permute-start(bf16[256,640]{1,0:T(8,128)(2,1)} %collective-permute-done.15.refs_20_), channel_id=1, source_target_pairs={{0,8},{4,20},{8,0},{12,28},{16,24},{20,4},{24,16},{28,12},{1,9},{5... | collective-permute-start | bytes 983048 | tf_op jit(solution)/shard_map/ppermute | solution.py:29
  67.1 13.0 %collective-permute-start.17 = (bf16[256,640]{1,0:T(8,128)(2,1)}, bf16[256,640]{1,0:T(8,128)(2,1)S(1)}, u32[]{:S(2)}, u32[]{:S(2)}) collective-permute-start(bf16[256,640]{1,0:T(8,128)(2,1)} %collective-permute-done.15.refs_20_), channel_id=1, source_target_pairs={{0,16},{4,12},{8,24},{12,4},{16,0},{20,28},{24,8},{28,20},{1,17},{... | collective-permute-start | bytes 983048 | tf_op jit(solution)/shard_map/ppermute | solution.py:29
  68.7 12.1 %collective-permute-start.12 = (bf16[256,640]{1,0:T(8,128)(2,1)}, bf16[256,640]{1,0:T(8,128)(2,1)S(1)}, u32[]{:S(2)}, u32[]{:S(2)}) collective-permute-start(bf16[256,640]{1,0:T(8,128)(2,1)} %copy-done.7), channel_id=1, source_target_pairs={{0,4},{4,0},{1,5},{5,1},{2,6},{6,2},{3,7},{7,3},{8,12},{12,8},{9,1... | collective-permute-start | bytes 983048 | tf_op jit(solution)/shard_map/ppermute | solution.py:23
  73.3 8.6 %collective-permute-start.10 = (bf16[256,640]{1,0:T(8,128)(2,1)}, bf16[256,640]{1,0:T(8,128)(2,1)S(1)}, u32[]{:S(2)}, u32[]{:S(2)}) collective-permute-start(bf16[256,640]{1,0:T(8,128)(2,1)} %copy-done.7), channel_id=1, source_target_pairs={{0,16},{4,12},{8,24},{12,4},{16,0},{20,28},{24,8},{28,20},{1,17},{... | collective-permute-start | bytes 983048 | tf_op jit(solution)/shard_map/ppermute | solution.py:29
  73.9 6.3 %collective-permute-start.13 = (bf16[256,640]{1,0:T(8,128)(2,1)}, bf16[256,640]{1,0:T(8,128)(2,1)S(1)}, u32[]{:S(2)}, u32[]{:S(2)}) collective-permute-start(bf16[256,640]{1,0:T(8,128)(2,1)} %copy-done.5), channel_id=1, source_target_pairs={{0,4},{4,0},{1,5},{5,1},{2,6},{6,2},{3,7},{7,3},{8,12},{12,8},{9,1... | collective-permute-start | bytes 983048 | tf_op jit(solution)/shard_map/ppermute | solution.py:23
  77.0 8.4 %collective-permute-start.18 = (bf16[256,640]{1,0:T(8,128)(2,1)}, bf16[256,640]{1,0:T(8,128)(2,1)S(1)}, u32[]{:S(2)}, u32[]{:S(2)}) collective-permute-start(bf16[256,640]{1,0:T(8,128)(2,1)} %collective-permute-done.16.refs_21_), channel_id=1, source_target_pairs={{0,16},{4,12},{8,24},{12,4},{16,0},{20,28},{24,8},{28,20},{1,17},{... | collective-permute-start | bytes 983048 | tf_op jit(solution)/shard_map/ppermute | solution.py:29
  78.5 8.6 %copy-start.2 = (bf16[256,2048]{1,0:T(8,128)(2,1)S(1)}, bf16[256,2048]{1,0:T(8,128)(2,1)}, u32[]{:S(2)}) copy-start(bf16[256,2048]{1,0:T(8,128)(2,1)} %refs_8_.1) | copy-start | bytes 3145732
  78.5 8.6 %copy-start.8 = (bf16[256,640]{1,0:T(8,128)(2,1)S(1)}, bf16[256,640]{1,0:T(8,128)(2,1)}, u32[]{:S(2)}) copy-start(bf16[256,640]{1,0:T(8,128)(2,1)} %copy-done.7) | copy-start | bytes 983044
  78.5 8.6 %copy-start.10 = (bf16[256,512]{1,0:T(8,128)(2,1)S(1)}, bf16[256,512]{1,0:T(8,128)(2,1)}, u32[]{:S(2)}) copy-start(bf16[256,512]{1,0:T(8,128)(2,1)} %copy-done.9) | copy-start | bytes 786436
  80.1 7.0 %copy-start.4 = (bf16[256,640]{1,0:T(8,128)(2,1)S(1)}, bf16[256,640]{1,0:T(8,128)(2,1)}, u32[]{:S(2)}) copy-start(bf16[256,640]{1,0:T(8,128)(2,1)} %copy-done.3) | copy-start | bytes 983044
  80.1 7.0 %copy-start.6 = (bf16[256,640]{1,0:T(8,128)(2,1)S(1)}, bf16[256,640]{1,0:T(8,128)(2,1)}, u32[]{:S(2)}) copy-start(bf16[256,640]{1,0:T(8,128)(2,1)} %copy-done.5) | copy-start | bytes 983044
  80.1 6.6 %collective-permute-start.20 = (bf16[256,640]{1,0:T(8,128)(2,1)}, bf16[256,640]{1,0:T(8,128)(2,1)S(1)}, u32[]{:S(2)}, u32[]{:S(2)}) collective-permute-start(bf16[256,640]{1,0:T(8,128)(2,1)} %collective-permute-done.16.refs_21_), channel_id=1, source_target_pairs={{0,4},{4,0},{1,5},{5,1},{2,6},{6,2},{3,7},{7,3},{8,12},{12,8},{9,1... | collective-permute-start | bytes 983048 | tf_op jit(solution)/shard_map/ppermute | solution.py:23
  80.2 6.5 %collective-permute-start.30 = (bf16[256,640]{1,0:T(8,128)(2,1)}, bf16[256,640]{1,0:T(8,128)(2,1)S(1)}, u32[]{:S(2)}, u32[]{:S(2)}) collective-permute-start(bf16[256,640]{1,0:T(8,128)(2,1)} %collective-permute-done.26.refs_31_), channel_id=1, source_target_pairs={{0,4},{4,0},{1,5},{5,1},{2,6},{6,2},{3,7},{7,3},{8,12},{12,8},{9,1... | collective-permute-start | bytes 983048 | tf_op jit(solution)/shard_map/ppermute | solution.py:23
  80.7 6.1 %collective-permute-start.21 = (bf16[256,640]{1,0:T(8,128)(2,1)S(1)}, bf16[256,640]{1,0:T(8,128)(2,1)S(1)}, u32[]{:S(2)}, u32[]{:S(2)}) collective-permute-start(bf16[256,640]{1,0:T(8,128)(2,1)S(1)} %collective-permute-done.17.refs_22_), channel_id=1, source_target_pairs={{0,4},{4,0},{1,5},{5,1},{2,6},{6,2},{3,7},{7,3},{8,12},{12,8},{9,1... | collective-permute-start | bytes 983048 | tf_op jit(solution)/shard_map/ppermute | solution.py:23
  81.9 4.9 %collective-permute-start.14 = (bf16[256,640]{1,0:T(8,128)(2,1)S(1)}, bf16[256,640]{1,0:T(8,128)(2,1)S(1)}, u32[]{:S(2)}, u32[]{:S(2)}) collective-permute-start(bf16[256,640]{1,0:T(8,128)(2,1)S(1)} %collective-permute-done.10.refs_15_), channel_id=1, source_target_pairs={{0,4},{4,0},{1,5},{5,1},{2,6},{6,2},{3,7},{7,3},{8,12},{12,8},{9,1... | collective-permute-start | bytes 983048 | tf_op jit(solution)/shard_map/ppermute | solution.py:23
  85.4 1.6 %collective-permute-start.22 = (bf16[256,640]{1,0:T(8,128)(2,1)S(1)}, bf16[256,640]{1,0:T(8,128)(2,1)S(1)}, u32[]{:S(2)}, u32[]{:S(2)}) collective-permute-start(bf16[256,640]{1,0:T(8,128)(2,1)S(1)} %collective-permute-done.18.refs_23_), channel_id=1, source_target_pairs={{0,4},{4,0},{1,5},{5,1},{2,6},{6,2},{3,7},{7,3},{8,12},{12,8},{9,1... | collective-permute-start | bytes 983048 | tf_op jit(solution)/shard_map/ppermute | solution.py:23
  87.7 0.9 copy-start.12
  88.7 0.9 copy-start.14
  (5 other events, 3.3 us)
